TPU v7x, 32 devices: a whole 2x2x4 slice. The times are simulated.
32 devices in a mesh: grp: 2 (over core), tm: 16 (over z, y, x).
Axes of the slice: x: 2, y: 2, z: 4, core: 2. Of those that a mesh axis runs over, the one named last changes fastest.
Arguments:
- x_start: float32 [512, 128], P(('grp', 'tm')), may hold values from -3 to 3
- y_start: float32 [512, 128], P('tm'), may hold values from 0 to 1
- cost: float32 [512, 128], P(('grp', 'tm')), may hold values from -6 to 6
- rhs: float32 [512, 128], P('tm'), may hold values from -6 to 6
- tiles: float32 [2048, 128, 128], P(('grp', 'tm')), may hold values from -0.375 to 0.375
- tile_rows: int32 [2048], P(('grp', 'tm')), may hold values from 0 to 511, as said below
- tile_cols: int32 [2048], P(('grp', 'tm')), may hold values from 0 to 511, as said below
- tile_count: int32 [32], P(('grp', 'tm')), may hold values from 1 to 64, as said below
- var_class: int32 [512, 128], P(('grp', 'tm')), may hold values from 0 to 7
- lower_table: float32 [8], replicated, may hold values from -1 to -0.2
- upper_table: float32 [8], replicated, may hold values from 0.2 to 1
Outputs:
- primal: float32 [512, 128], P(('grp', 'tm'))
- dual: float32 [512, 128], P('tm')
- primal_mean: float32 [512, 128], P(('grp', 'tm'))
- dual_mean: float32 [512, 128], P('tm')
Inputs may be any that keep to these rules, and one draw needn't show every extreme that they name: `tile_cols`: the tile slots of device d (slots d * 64 to (d + 1) * 64 - 1) name only that device's own column blocks d * 16 to (d + 1) * 16 - 1. `tile_rows`: the tile slots of device d = g * 16 + t name only row blocks of time blocks t - 1, t and t + 1 (rows k * 32 to (k + 1) * 32 - 1 belong to time block k). Only the first tile_count[d] slots of device d are live; some device has all 64 slots live.
All inputs are finite; a program needn't handle non-finite values.
Results may differ from a plain program's by a relative error of at most 0.0001.
Values sent between devices are 32-bit elements; how exact they have to be, the bound alone decides.
No kernel may reach another device: no remote copies, remote signals or barrier semaphores. Data moves between devices by JAX's collectives and lax.ppermute only.
A program may use at most 64 MiB of HBM per device.

v0:
```python
import jax
import jax.numpy as jnp
from jax import lax
from jax.sharding import PartitionSpec as P

ITERS = 2
primal_step = 0.6
dual_step = 0.6


def with_halo(block, sides, width):
    for axis, dim in sides:
        count = lax.axis_size(axis)
        forward = [(i, i + 1) for i in range(count - 1)]
        backward = [(target, source) for source, target in forward]
        low = lax.ppermute(
            lax.slice_in_dim(block, block.shape[dim] - width, None, axis=dim), axis, forward
        )
        high = lax.ppermute(lax.slice_in_dim(block, 0, width, axis=dim), axis, backward)
        block = jnp.concatenate([low, block, high], axis=dim)
    return block


def shifted(block, axis, distance):
    devices = range(lax.axis_size(axis))
    route = [(i - distance, i) for i in devices if i - distance in devices]
    return lax.ppermute(block, axis, route)


def dual_update(dual_part, rhs_part, image_part):
    return jnp.maximum(dual_part + dual_step * (rhs_part - image_part), 0.0)


def body(
    x_start,
    y_start,
    cost,
    rhs,
    tiles,
    tile_rows,
    tile_cols,
    tile_count,
    var_class,
    lower_table,
    upper_table,
):
    tile_total = tiles.shape[0]
    col_blocks = x_start.shape[0]
    row_blocks = y_start.shape[0]
    time_devices = lax.axis_size("tm")
    time_index = lax.axis_index("tm")
    device_index = lax.axis_index("grp") * time_devices + time_index
    local_cols = tile_cols - device_index * col_blocks
    live_mask = (jnp.arange(tile_total) < tile_count[0]).astype(jnp.float32)[:, None]
    col_select = (local_cols[:, None] == jnp.arange(col_blocks)[None, :]).astype(jnp.float32)
    lower_bound = jnp.zeros(x_start.shape, jnp.float32)
    upper_bound = jnp.zeros(x_start.shape, jnp.float32)
    for class_id in range(lower_table.shape[0]):
        lower_bound = jnp.where(var_class == class_id, lower_table[class_id], lower_bound)
        upper_bound = jnp.where(var_class == class_id, upper_table[class_id], upper_bound)
    window_first = (time_index - 1) * row_blocks
    row_select = (
        (tile_rows - window_first)[:, None] == jnp.arange(3 * row_blocks)[None, :]
    ).astype(jnp.float32)
    dual_view = with_halo(y_start, (("tm", 0),), row_blocks)
    primal = x_start
    dual = y_start
    primal_total = jnp.zeros_like(x_start)
    dual_total = jnp.zeros_like(y_start)
    for iteration in range(ITERS):
        dual_picked = jnp.dot(row_select, dual_view, precision=lax.Precision.HIGHEST)
        backward = (
            jnp.einsum("nrc,nr->nc", tiles, dual_picked, precision=lax.Precision.HIGHEST)
            * live_mask
        )
        adjoint_part = jnp.dot(col_select.T, backward, precision=lax.Precision.HIGHEST)
        moved = primal - primal_step * (cost - adjoint_part)
        primal_next = jnp.minimum(jnp.maximum(moved, lower_bound), upper_bound)
        extrapolated = 2.0 * primal_next - primal
        primal_picked = jnp.dot(col_select, extrapolated, precision=lax.Precision.HIGHEST)
        forward = (
            jnp.einsum("nrc,nc->nr", tiles, primal_picked, precision=lax.Precision.HIGHEST)
            * live_mask
        )
        window_terms = jnp.dot(row_select.T, forward, precision=lax.Precision.HIGHEST)
        summed = lax.psum(window_terms, "grp")
        from_above = shifted(summed[:row_blocks], "tm", -1)
        from_below = shifted(summed[2 * row_blocks :], "tm", 1)
        image_slab = summed[row_blocks : 2 * row_blocks] + from_above + from_below
        dual_next = dual_update(dual, rhs, image_slab)
        if iteration + 1 < ITERS:
            dual_view = with_halo(dual_next, (("tm", 0),), row_blocks)
        primal_total = primal_total + primal_next
        dual_total = dual_total + dual_next
        primal = primal_next
        dual = dual_next
    return (primal, dual, primal_total / ITERS, dual_total / ITERS)


def solution(mesh):
    return jax.shard_map(
        body,
        mesh=mesh,
        in_specs=(
            P(("grp", "tm"), None),
            P("tm", None),
            P(("grp", "tm"), None),
            P("tm", None),
            P(("grp", "tm"), None, None),
            P(("grp", "tm")),
            P(("grp", "tm")),
            P(("grp", "tm")),
            P(("grp", "tm"), None),
            P(),
            P(),
        ),
        out_specs=(P(("grp", "tm"), None), P("tm", None), P(("grp", "tm"), None), P("tm", None)),
        check_vma=False,
    )
```

profile of v0, /device:TPU:16, one launch (start us, length us, event | category | flops | bytes accessed | tf_op | source)
XLA Modules:
  0.0 100.7 jit_solution(15821462959131894350)
XLA Ops:
  0.7 4.4 %collective-permute-start.1 = (f32[32,128]{1,0:T(8,128)}, f32[32,128]{1,0:T(8,128)S(1)}, u32[]{:S(2)}, u32[]{:S(2)}) collective-permute-start(f32[32,128]{1,0:T(8,128)} %param.12), channel_id=1, source_target_pairs={{1,0},{2,1},{3,2},{4,3},{5,4},{6,5},{7,6},{8,7},{9,8},{10,9},{11,1... | collective-permute-start | bytes 49160 | tf_op jit(solution)/shard_map/ppermute | solution.py:19
  5.0 1.9 %collective-permute-start = (f32[32,128]{1,0:T(8,128)}, f32[32,128]{1,0:T(8,128)S(1)}, u32[]{:S(2)}, u32[]{:S(2)}) collective-permute-start(f32[32,128]{1,0:T(8,128)} %param.12), channel_id=1, source_target_pairs={{0,1},{1,2},{2,3},{3,4},{4,5},{5,6},{6,7},{7,8},{8,9},{9,10},{10,1... | collective-permute-start | bytes 49160 | tf_op jit(solution)/shard_map/ppermute | solution.py:16
  7.6 1.6 %fusion.64 = (f32[1]{0:T(128)}, f32[1]{0:T(128)}, f32[1]{0:T(128)}, f32[1]{0:T(128)}, f32[1]{0:T(128)}, /*index=5*/f32[1]{0:T(128)}, f32[1]{0:T(128)}, f32[1]{0:T(128)}) fusion(f32[8]{0:T(128)} %param.20), kind=kLoop, calls=%fused_computation.84 | loop fusion | bytes 64 | tf_op jit(solution)/shard_map/slice | solution.py:59
  9.3 1.6 %fusion.63 = (f32[1]{0:T(128)}, f32[1]{0:T(128)}, f32[1]{0:T(128)}, f32[1]{0:T(128)}, f32[1]{0:T(128)}, /*index=5*/f32[1]{0:T(128)}, f32[1]{0:T(128)}, f32[1]{0:T(128)}) fusion(f32[8]{0:T(128)} %param.21), kind=kLoop, calls=%fused_computation.83 | loop fusion | bytes 64 | tf_op jit(solution)/shard_map/slice | solution.py:60
  11.6 0.8 broadcast_subtract_fusion.1
  12.4 0.8 broadcast_subtract_fusion
  13.3 0.9 fusion.8
  14.2 5.3 %fusion.65 = f32[64,1,128]{2,1,0:T(1,128)S(1)} fusion(f32[64,128,1]{1,2,0:T(1,128)S(1)} %bitcast.46, f32[64,128,128]{2,1,0:T(8,128)} %param.15), kind=kOutput, calls=%fused_computation.85 | convolution fusion | flops 12582912 | bytes 4259840 | tf_op jit(solution)/shard_map/nrc,nr->nc/dot_general | solution.py:73
  19.5 10.4 %fusion.7 = f32[16,128]{1,0:T(8,128)S(1)} fusion(f32[16,128]{1,0:T(8,128)S(1)} %copy-done.4, f32[16,128]{1,0:T(8,128)S(1)} %copy-done.5, f32[64,128]{1,0:T(8,128)S(1)} %bitcast.49, f32[64]{0:T(128)S(1)} %compare_convert_fusion, s32[64]{0:T(128)S(1)} %broadcast_subtract_fusion.1, pred[16,128]{1,0:T(8,128)(4,1)S(1)} %get-tuple-element.16, ...), kind=kOutput, calls=%fused_computation.9 | convolution fusion | flops 1625088 | bytes 74304 | tf_op jit(solution)/shard_map/dot_general | solution.py:76
  30.2 6.6 %fusion.66 = f32[64,1,128]{2,1,0:T(1,128)S(1)} fusion(f32[64,128,1]{1,2,0:T(1,128)S(1)} %bitcast.53, f32[64,128,128]{2,1,0:T(8,128)S(1)} %copy-done), kind=kOutput, calls=%fused_computation.86 | convolution fusion | flops 12582912 | bytes 4259840 | tf_op jit(solution)/shard_map/nrc,nc->nr/dot_general | solution.py:82
  37.1 3.5 %psum.14 = f32[96,128]{1,0:T(8,128)S(1)} all-reduce(f32[96,128]{1,0:T(8,128)S(1)} %fusion.23), channel_id=1, replica_groups=mesh['grp'=2,'tm'=16] {'grp'}, use_global_device_ids=true, to_apply=%region_0.1 | all-reduce | flops 12288 | bytes 98304 | tf_op jit(solution)/shard_map/psum | solution.py:86
  40.7 6.0 %collective-permute-start.2 = (f32[32,128]{1,0:T(8,128)S(1)}, f32[32,128]{1,0:T(8,128)S(1)}, u32[]{:S(2)}, u32[]{:S(2)}) collective-permute-start(f32[32,128]{1,0:T(8,128)S(1)} %get-tuple-element.8), channel_id=1, source_target_pairs={{1,0},{2,1},{3,2},{4,3},{5,4},{6,5},{7,6},{8,7},{9,8},{10,9},{11,1... | collective-permute-start | bytes 49160 | tf_op jit(solution)/shard_map/ppermute | solution.py:27
  46.6 1.9 %collective-permute-start.3 = (f32[32,128]{1,0:T(8,128)S(1)}, f32[32,128]{1,0:T(8,128)S(1)}, u32[]{:S(2)}, u32[]{:S(2)}) collective-permute-start(f32[32,128]{1,0:T(8,128)S(1)} %get-tuple-element.9), channel_id=1, source_target_pairs={{0,1},{1,2},{2,3},{3,4},{4,5},{5,6},{6,7},{7,8},{8,9},{9,10},{10,1... | collective-permute-start | bytes 49160 | tf_op jit(solution)/shard_map/ppermute | solution.py:27
  48.6 5.5 %collective-permute-done.3 = f32[32,128]{1,0:T(8,128)S(1)} collective-permute-done((f32[32,128]{1,0:T(8,128)S(1)}, f32[32,128]{1,0:T(8,128)S(1)}, u32[]{:S(2)}, u32[]{:S(2)}) %collective-permute-start.3) | collective-permute-done | bytes 16416 | tf_op jit(solution)/shard_map/ppermute | solution.py:27
  54.1 1.9 %collective-permute-start.5 = (f32[32,128]{1,0:T(8,128)S(1)}, f32[32,128]{1,0:T(8,128)S(1)}, u32[]{:S(2)}, u32[]{:S(2)}) collective-permute-start(f32[32,128]{1,0:T(8,128)S(1)} %fusion.37), channel_id=1, source_target_pairs={{1,0},{2,1},{3,2},{4,3},{5,4},{6,5},{7,6},{8,7},{9,8},{10,9},{11,1... | collective-permute-start | bytes 49160 | tf_op jit(solution)/shard_map/ppermute | solution.py:19
  56.0 4.1 %collective-permute-start.4 = (f32[32,128]{1,0:T(8,128)S(1)}, f32[32,128]{1,0:T(8,128)S(1)}, u32[]{:S(2)}, u32[]{:S(2)}) collective-permute-start(f32[32,128]{1,0:T(8,128)S(1)} %fusion.37), channel_id=1, source_target_pairs={{0,1},{1,2},{2,3},{3,4},{4,5},{5,6},{6,7},{7,8},{8,9},{9,10},{10,1... | collective-permute-start | bytes 49160 | tf_op jit(solution)/shard_map/ppermute | solution.py:16
  60.1 3.3 %collective-permute-done.4 = f32[32,128]{1,0:T(8,128)S(1)} collective-permute-done((f32[32,128]{1,0:T(8,128)S(1)}, f32[32,128]{1,0:T(8,128)S(1)}, u32[]{:S(2)}, u32[]{:S(2)}) %collective-permute-start.4) | collective-permute-done | bytes 16416 | tf_op jit(solution)/shard_map/ppermute | solution.py:16
  63.7 5.3 %fusion.67 = f32[64,1,128]{2,1,0:T(1,128)S(1)} fusion(f32[64,128,1]{1,2,0:T(1,128)S(1)} %bitcast.47, f32[64,128,128]{2,1,0:T(8,128)} %param.15), kind=kOutput, calls=%fused_computation.87 | convolution fusion | flops 12582912 | bytes 4259840 | tf_op jit(solution)/shard_map/nrc,nr->nc/dot_general | solution.py:73
  68.9 11.1 %add_multiply_fusion.1 = (f32[16,128]{1,0:T(8,128)}, f32[16,128]{1,0:T(8,128)S(1)}) fusion(f32[16,128]{1,0:T(8,128)S(1)} %fusion.7, pred[16,128]{1,0:T(8,128)(4,1)S(1)} %get-tuple-element.16, pred[16,128]{1,0:T(8,128)(4,1)S(1)} %get-tuple-element.15, pred[16,128]{1,0:T(8,128)(4,1)S(1)} %get-tuple-element.14, pred[16,128]{1,0:T(8,128)(4,1)S(1)} %get-tuple-element.13, ...), kind=kOutput, calls=%fused_computation.57 | convolution fusion | flops 1629184 | bytes 82496 | tf_op jit(solution)/shard_map/dot_general | solution.py:76
  80.2 6.6 %fusion.68 = f32[64,1,128]{2,1,0:T(1,128)S(1)} fusion(f32[64,128,1]{1,2,0:T(1,128)S(1)} %bitcast.51, f32[64,128,128]{2,1,0:T(8,128)S(1)} %copy-done.1), kind=kOutput, calls=%fused_computation.88 | convolution fusion | flops 12582912 | bytes 4259840 | tf_op jit(solution)/shard_map/nrc,nc->nr/dot_general | solution.py:82
  87.1 3.5 %psum.15 = f32[96,128]{1,0:T(8,128)S(1)} all-reduce(f32[96,128]{1,0:T(8,128)S(1)} %fusion.20), channel_id=1, replica_groups=mesh['grp'=2,'tm'=16] {'grp'}, use_global_device_ids=true, to_apply=%region_1.2 | all-reduce | flops 12288 | bytes 98304 | tf_op jit(solution)/shard_map/psum | solution.py:86
  90.7 1.9 %collective-permute-start.6 = (f32[32,128]{1,0:T(8,128)S(1)}, f32[32,128]{1,0:T(8,128)S(1)}, u32[]{:S(2)}, u32[]{:S(2)}) collective-permute-start(f32[32,128]{1,0:T(8,128)S(1)} %get-tuple-element.6), channel_id=1, source_target_pairs={{1,0},{2,1},{3,2},{4,3},{5,4},{6,5},{7,6},{8,7},{9,8},{10,9},{11,1... | collective-permute-start | bytes 49160 | tf_op jit(solution)/shard_map/ppermute | solution.py:27
  92.6 3.9 %collective-permute-start.7 = (f32[32,128]{1,0:T(8,128)S(1)}, f32[32,128]{1,0:T(8,128)S(1)}, u32[]{:S(2)}, u32[]{:S(2)}) collective-permute-start(f32[32,128]{1,0:T(8,128)S(1)} %get-tuple-element.7), channel_id=1, source_target_pairs={{0,1},{1,2},{2,3},{3,4},{4,5},{5,6},{6,7},{7,8},{8,9},{9,10},{10,1... | collective-permute-start | bytes 49160 | tf_op jit(solution)/shard_map/ppermute | solution.py:27
  96.6 3.5 %collective-permute-done.7 = f32[32,128]{1,0:T(8,128)S(1)} collective-permute-done((f32[32,128]{1,0:T(8,128)S(1)}, f32[32,128]{1,0:T(8,128)S(1)}, u32[]{:S(2)}, u32[]{:S(2)}) %collective-permute-start.7) | collective-permute-done | bytes 16416 | tf_op jit(solution)/shard_map/ppermute | solution.py:27
  (30 shorter events, 2.6 us)
Async XLA Ops:
  0.6 18.9 %copy-start.5 = (f32[16,128]{1,0:T(8,128)S(1)}, f32[16,128]{1,0:T(8,128)}, u32[]{:S(2)}) copy-start(f32[16,128]{1,0:T(8,128)} %param.13) | copy-start | bytes 24580
  0.6 18.9 %copy-start.4 = (f32[16,128]{1,0:T(8,128)S(1)}, f32[16,128]{1,0:T(8,128)}, u32[]{:S(2)}) copy-start(f32[16,128]{1,0:T(8,128)} %param.11) | copy-start | bytes 24580
  0.7 12.6 %collective-permute-start.1 = (f32[32,128]{1,0:T(8,128)}, f32[32,128]{1,0:T(8,128)S(1)}, u32[]{:S(2)}, u32[]{:S(2)}) collective-permute-start(f32[32,128]{1,0:T(8,128)} %param.12), channel_id=1, source_target_pairs={{1,0},{2,1},{3,2},{4,3},{5,4},{6,5},{7,6},{8,7},{9,8},{10,9},{11,1... | collective-permute-start | bytes 49160 | tf_op jit(solution)/shard_map/ppermute | solution.py:19
  5.0 8.2 %collective-permute-start = (f32[32,128]{1,0:T(8,128)}, f32[32,128]{1,0:T(8,128)S(1)}, u32[]{:S(2)}, u32[]{:S(2)}) collective-permute-start(f32[32,128]{1,0:T(8,128)} %param.12), channel_id=1, source_target_pairs={{0,1},{1,2},{2,3},{3,4},{4,5},{5,6},{6,7},{7,8},{8,9},{9,10},{10,1... | collective-permute-start | bytes 49160 | tf_op jit(solution)/shard_map/ppermute | solution.py:16
  11.6 18.6 %copy-start = (f32[64,128,128]{2,1,0:T(8,128)S(1)}, f32[64,128,128]{2,1,0:T(8,128)}, u32[]{:S(2)}) copy-start(f32[64,128,128]{2,1,0:T(8,128)} %param.15) | copy-start | bytes 12582916
  14.2 39.9 %copy-start.2 = (f32[32,128]{1,0:T(8,128)S(1)}, f32[32,128]{1,0:T(8,128)}, u32[]{:S(2)}) copy-start(f32[32,128]{1,0:T(8,128)} %param.12) | copy-start | bytes 49156
  14.2 39.9 %copy-start.3 = (f32[32,128]{1,0:T(8,128)S(1)}, f32[32,128]{1,0:T(8,128)}, u32[]{:S(2)}) copy-start(f32[32,128]{1,0:T(8,128)} %param.14) | copy-start | bytes 49156
  40.6 39.6 %copy-start.1 = (f32[64,128,128]{2,1,0:T(8,128)S(1)}, f32[64,128,128]{2,1,0:T(8,128)}, u32[]{:S(2)}) copy-start(f32[64,128,128]{2,1,0:T(8,128)} %param.15) | copy-start | bytes 12582916
  40.7 7.9 %collective-permute-start.2 = (f32[32,128]{1,0:T(8,128)S(1)}, f32[32,128]{1,0:T(8,128)S(1)}, u32[]{:S(2)}, u32[]{:S(2)}) collective-permute-start(f32[32,128]{1,0:T(8,128)S(1)} %get-tuple-element.8), channel_id=1, source_target_pairs={{1,0},{2,1},{3,2},{4,3},{5,4},{6,5},{7,6},{8,7},{9,8},{10,9},{11,1... | collective-permute-start | bytes 49160 | tf_op jit(solution)/shard_map/ppermute | solution.py:27
  46.6 7.4 %collective-permute-start.3 = (f32[32,128]{1,0:T(8,128)S(1)}, f32[32,128]{1,0:T(8,128)S(1)}, u32[]{:S(2)}, u32[]{:S(2)}) collective-permute-start(f32[32,128]{1,0:T(8,128)S(1)} %get-tuple-element.9), channel_id=1, source_target_pairs={{0,1},{1,2},{2,3},{3,4},{4,5},{5,6},{6,7},{7,8},{8,9},{9,10},{10,1... | collective-permute-start | bytes 49160 | tf_op jit(solution)/shard_map/ppermute | solution.py:27
  54.1 6.0 %collective-permute-start.5 = (f32[32,128]{1,0:T(8,128)S(1)}, f32[32,128]{1,0:T(8,128)S(1)}, u32[]{:S(2)}, u32[]{:S(2)}) collective-permute-start(f32[32,128]{1,0:T(8,128)S(1)} %fusion.37), channel_id=1, source_target_pairs={{1,0},{2,1},{3,2},{4,3},{5,4},{6,5},{7,6},{8,7},{9,8},{10,9},{11,1... | collective-permute-start | bytes 49160 | tf_op jit(solution)/shard_map/ppermute | solution.py:19
  56.0 7.4 %collective-permute-start.4 = (f32[32,128]{1,0:T(8,128)S(1)}, f32[32,128]{1,0:T(8,128)S(1)}, u32[]{:S(2)}, u32[]{:S(2)}) collective-permute-start(f32[32,128]{1,0:T(8,128)S(1)} %fusion.37), channel_id=1, source_target_pairs={{0,1},{1,2},{2,3},{3,4},{4,5},{5,6},{6,7},{7,8},{8,9},{9,10},{10,1... | collective-permute-start | bytes 49160 | tf_op jit(solution)/shard_map/ppermute | solution.py:16
  80.0 20.7 %copy-start.6 = (f32[16,128]{1,0:T(8,128)}, f32[16,128]{1,0:T(8,128)S(1)}, u32[]{:S(2)}) copy-start(f32[16,128]{1,0:T(8,128)S(1)} %get-tuple-element.35) | copy-start | bytes 24580
  90.7 5.9 %collective-permute-start.6 = (f32[32,128]{1,0:T(8,128)S(1)}, f32[32,128]{1,0:T(8,128)S(1)}, u32[]{:S(2)}, u32[]{:S(2)}) collective-permute-start(f32[32,128]{1,0:T(8,128)S(1)} %get-tuple-element.6), channel_id=1, source_target_pairs={{1,0},{2,1},{3,2},{4,3},{5,4},{6,5},{7,6},{8,7},{9,8},{10,9},{11,1... | collective-permute-start | bytes 49160 | tf_op jit(solution)/shard_map/ppermute | solution.py:27
  92.6 7.4 %collective-permute-start.7 = (f32[32,128]{1,0:T(8,128)S(1)}, f32[32,128]{1,0:T(8,128)S(1)}, u32[]{:S(2)}, u32[]{:S(2)}) collective-permute-start(f32[32,128]{1,0:T(8,128)S(1)} %get-tuple-element.7), channel_id=1, source_target_pairs={{0,1},{1,2},{2,3},{3,4},{4,5},{5,6},{6,7},{7,8},{8,9},{9,10},{10,1... | collective-permute-start | bytes 49160 | tf_op jit(solution)/shard_map/ppermute | solution.py:27
where the time goes:
time: 101 us
  matrix products  47.4 us (47%)
  starting transfers between devices  26.1 us (26%)
  waiting for transfers between devices  12.3 us (12%)
  blocking collectives  7.06 us (7%)
  local copies, waits for them, and re-layouts  3.31 us (3%)
  other arithmetic  2.99 us (3%)
  between operations  1.53 us (2%)
    dot_general x2, matrix products, body(): jnp.dot(col_select.T, backward, precision=lax.Precision.HIGHEST)  21.5 us
    ppermute x4, starting transfers between devices, shifted(): return lax.ppermute(block, axis, route)  13.7 us
    dot_general x2, matrix products, body(): jnp.einsum('nrc,nc->nr', tiles, primal_picked, precision=lax.Precision.HI...  13.2 us
    dot_general x2, matrix products, body(): jnp.einsum('nrc,nr->nc', tiles, dual_picked, precision=lax.Precision.HIGH...  10.6 us
    ppermute x4, waiting for transfers between devices, shifted(): return lax.ppermute(block, axis, route)  8.99 us
    psum x2, blocking collectives, body(): summed = lax.psum(window_terms, 'grp')  7.06 us
    ppermute x2, starting transfers between devices, with_halo(): lax.ppermute(lax.slice_in_dim(block, 0, width, axis=dim), axis, backward)  6.3 us
    ppermute x2, starting transfers between devices, with_halo(): lax.ppermute(lax.slice_in_dim(block, block.shape[dim] - width, None, axis...  6.03 us
  transfers between devices with their start and end apart: 8, of which 3 were waited for; matrix products, arithmetic and copies ran while one was open for 6% of the time, Pallas kernels for 0%

commit v1 on v0

--- a/solution.py
+++ b/solution.py
@@ -83,7 +83,8 @@
             * live_mask
         )
         window_terms = jnp.dot(row_select.T, forward, precision=lax.Precision.HIGHEST)
-        summed = lax.psum(window_terms, "grp")
+        parts = lax.all_gather(window_terms, "grp", axis=0, tiled=False)
+        summed = parts.sum(axis=0)
         from_above = shifted(summed[:row_blocks], "tm", -1)
         from_below = shifted(summed[2 * row_blocks :], "tm", 1)
         image_slab = summed[row_blocks : 2 * row_blocks] + from_above + from_below

time: 101 us -> 98.1 us (0.971)
  blocking collectives: 7.06 us -> 3.75 us
    psum x2 -> x0, blocking collectives: 7.06 us -> none  [body(): summed = lax.psum(window_terms, 'grp')]
    all_gather x0 -> x2, blocking collectives: none -> 3.75 us  [body(): parts = lax.all_gather(window_terms, 'grp', axis=0, tiled=False)]
where the time goes in v1:
time: 98.1 us; the launch traced here: 97.4 us
  matrix products  47.4 us (48%)
  starting transfers between devices  26.1 us (27%)
  waiting for transfers between devices  12.3 us (13%)
  blocking collectives  3.75 us (4%)
  local copies, waits for them, and re-layouts  3.31 us (3%)
  other arithmetic  3 us (3%)
  between operations  1.52 us (2%)
    dot_general x2, matrix products, body(): jnp.dot(col_select.T, backward, precision=lax.Precision.HIGHEST)  21.5 us
    ppermute x4, starting transfers between devices, shifted(): return lax.ppermute(block, axis, route)  13.7 us
    dot_general x2, matrix products, body(): jnp.einsum('nrc,nc->nr', tiles, primal_picked, precision=lax.Precision.HI...  13.2 us
    dot_general x2, matrix products, body(): jnp.einsum('nrc,nr->nc', tiles, dual_picked, precision=lax.Precision.HIGH...  10.6 us
    ppermute x4, waiting for transfers between devices, shifted(): return lax.ppermute(block, axis, route)  8.99 us
    ppermute x2, starting transfers between devices, with_halo(): lax.ppermute(lax.slice_in_dim(block, 0, width, axis=dim), axis, backward)  6.3 us
    ppermute x2, starting transfers between devices, with_halo(): lax.ppermute(lax.slice_in_dim(block, block.shape[dim] - width, None, axis...  6.03 us
    all_gather x2, blocking collectives, body(): parts = lax.all_gather(window_terms, 'grp', axis=0, tiled=False)  3.75 us
  transfers between devices with their start and end apart: 8, of which 3 were waited for; matrix products, arithmetic and copies ran while one was open for 6% of the time, Pallas kernels for 0%

profile of v1, /device:TPU:16, one launch (start us, length us, event | category | flops | bytes accessed | tf_op | source)
XLA Modules:
  0.0 97.4 jit_solution(4004970547573323741)
XLA Ops:
  0.7 4.4 %collective-permute-start.1 = (f32[32,128]{1,0:T(8,128)}, f32[32,128]{1,0:T(8,128)S(1)}, u32[]{:S(2)}, u32[]{:S(2)}) collective-permute-start(f32[32,128]{1,0:T(8,128)} %param.12), channel_id=1, source_target_pairs={{1,0},{2,1},{3,2},{4,3},{5,4},{6,5},{7,6},{8,7},{9,8},{10,9},{11,1... | collective-permute-start | bytes 49160 | tf_op jit(solution)/shard_map/ppermute | solution.py:19
  5.0 1.9 %collective-permute-start = (f32[32,128]{1,0:T(8,128)}, f32[32,128]{1,0:T(8,128)S(1)}, u32[]{:S(2)}, u32[]{:S(2)}) collective-permute-start(f32[32,128]{1,0:T(8,128)} %param.12), channel_id=1, source_target_pairs={{0,1},{1,2},{2,3},{3,4},{4,5},{5,6},{6,7},{7,8},{8,9},{9,10},{10,1... | collective-permute-start | bytes 49160 | tf_op jit(solution)/shard_map/ppermute | solution.py:16
  7.6 1.6 %fusion.64 = (f32[1]{0:T(128)}, f32[1]{0:T(128)}, f32[1]{0:T(128)}, f32[1]{0:T(128)}, f32[1]{0:T(128)}, /*index=5*/f32[1]{0:T(128)}, f32[1]{0:T(128)}, f32[1]{0:T(128)}) fusion(f32[8]{0:T(128)} %param.20), kind=kLoop, calls=%fused_computation.84 | loop fusion | bytes 64 | tf_op jit(solution)/shard_map/slice | solution.py:59
  9.3 1.6 %fusion.63 = (f32[1]{0:T(128)}, f32[1]{0:T(128)}, f32[1]{0:T(128)}, f32[1]{0:T(128)}, f32[1]{0:T(128)}, /*index=5*/f32[1]{0:T(128)}, f32[1]{0:T(128)}, f32[1]{0:T(128)}) fusion(f32[8]{0:T(128)} %param.21), kind=kLoop, calls=%fused_computation.83 | loop fusion | bytes 64 | tf_op jit(solution)/shard_map/slice | solution.py:60
  11.6 0.8 broadcast_subtract_fusion.1
  12.4 0.8 broadcast_subtract_fusion
  13.3 0.9 fusion.8
  14.2 5.3 %fusion.65 = f32[64,1,128]{2,1,0:T(1,128)S(1)} fusion(f32[64,128,1]{1,2,0:T(1,128)S(1)} %bitcast.50, f32[64,128,128]{2,1,0:T(8,128)} %param.15), kind=kOutput, calls=%fused_computation.85 | convolution fusion | flops 12582912 | bytes 4259840 | tf_op jit(solution)/shard_map/nrc,nr->nc/dot_general | solution.py:73
  19.5 10.4 %fusion.7 = f32[16,128]{1,0:T(8,128)S(1)} fusion(f32[16,128]{1,0:T(8,128)S(1)} %copy-done.4, f32[16,128]{1,0:T(8,128)S(1)} %copy-done.5, f32[64,128]{1,0:T(8,128)S(1)} %bitcast.53, f32[64]{0:T(128)S(1)} %compare_convert_fusion, s32[64]{0:T(128)S(1)} %broadcast_subtract_fusion.1, pred[16,128]{1,0:T(8,128)(4,1)S(1)} %get-tuple-element.16, ...), kind=kOutput, calls=%fused_computation.9 | convolution fusion | flops 1625088 | bytes 74304 | tf_op jit(solution)/shard_map/dot_general | solution.py:76
  30.2 6.6 %fusion.66 = f32[64,1,128]{2,1,0:T(1,128)S(1)} fusion(f32[64,128,1]{1,2,0:T(1,128)S(1)} %bitcast.57, f32[64,128,128]{2,1,0:T(8,128)S(1)} %copy-done), kind=kOutput, calls=%fused_computation.86 | convolution fusion | flops 12582912 | bytes 4259840 | tf_op jit(solution)/shard_map/nrc,nc->nr/dot_general | solution.py:82
  37.1 1.9 %all-gather = f32[192,128]{1,0:T(8,128)S(1)} all-gather(f32[96,128]{1,0:T(8,128)S(1)} %fusion.23), channel_id=2, replica_groups=mesh['grp'=2,'tm'=16] {'grp'}, dimensions={0}, use_global_device_ids=true | all-gather | bytes 147456 | tf_op jit(solution)/shard_map/all_gather | solution.py:86
  39.0 6.0 %collective-permute-start.2 = (f32[32,128]{1,0:T(8,128)S(1)}, f32[32,128]{1,0:T(8,128)S(1)}, u32[]{:S(2)}, u32[]{:S(2)}) collective-permute-start(f32[32,128]{1,0:T(8,128)S(1)} %get-tuple-element.8), channel_id=1, source_target_pairs={{1,0},{2,1},{3,2},{4,3},{5,4},{6,5},{7,6},{8,7},{9,8},{10,9},{11,1... | collective-permute-start | bytes 49160 | tf_op jit(solution)/shard_map/ppermute | solution.py:27
  45.0 1.9 %collective-permute-start.3 = (f32[32,128]{1,0:T(8,128)S(1)}, f32[32,128]{1,0:T(8,128)S(1)}, u32[]{:S(2)}, u32[]{:S(2)}) collective-permute-start(f32[32,128]{1,0:T(8,128)S(1)} %get-tuple-element.9), channel_id=1, source_target_pairs={{0,1},{1,2},{2,3},{3,4},{4,5},{5,6},{6,7},{7,8},{8,9},{9,10},{10,1... | collective-permute-start | bytes 49160 | tf_op jit(solution)/shard_map/ppermute | solution.py:27
  46.9 5.5 %collective-permute-done.3 = f32[32,128]{1,0:T(8,128)S(1)} collective-permute-done((f32[32,128]{1,0:T(8,128)S(1)}, f32[32,128]{1,0:T(8,128)S(1)}, u32[]{:S(2)}, u32[]{:S(2)}) %collective-permute-start.3) | collective-permute-done | bytes 16416 | tf_op jit(solution)/shard_map/ppermute | solution.py:27
  52.4 1.9 %collective-permute-start.5 = (f32[32,128]{1,0:T(8,128)S(1)}, f32[32,128]{1,0:T(8,128)S(1)}, u32[]{:S(2)}, u32[]{:S(2)}) collective-permute-start(f32[32,128]{1,0:T(8,128)S(1)} %fusion.37), channel_id=1, source_target_pairs={{1,0},{2,1},{3,2},{4,3},{5,4},{6,5},{7,6},{8,7},{9,8},{10,9},{11,1... | collective-permute-start | bytes 49160 | tf_op jit(solution)/shard_map/ppermute | solution.py:19
  54.4 4.1 %collective-permute-start.4 = (f32[32,128]{1,0:T(8,128)S(1)}, f32[32,128]{1,0:T(8,128)S(1)}, u32[]{:S(2)}, u32[]{:S(2)}) collective-permute-start(f32[32,128]{1,0:T(8,128)S(1)} %fusion.37), channel_id=1, source_target_pairs={{0,1},{1,2},{2,3},{3,4},{4,5},{5,6},{6,7},{7,8},{8,9},{9,10},{10,1... | collective-permute-start | bytes 49160 | tf_op jit(solution)/shard_map/ppermute | solution.py:16
  58.5 3.3 %collective-permute-done.4 = f32[32,128]{1,0:T(8,128)S(1)} collective-permute-done((f32[32,128]{1,0:T(8,128)S(1)}, f32[32,128]{1,0:T(8,128)S(1)}, u32[]{:S(2)}, u32[]{:S(2)}) %collective-permute-start.4) | collective-permute-done | bytes 16416 | tf_op jit(solution)/shard_map/ppermute | solution.py:16
  62.0 5.3 %fusion.67 = f32[64,1,128]{2,1,0:T(1,128)S(1)} fusion(f32[64,128,1]{1,2,0:T(1,128)S(1)} %bitcast.51, f32[64,128,128]{2,1,0:T(8,128)} %param.15), kind=kOutput, calls=%fused_computation.87 | convolution fusion | flops 12582912 | bytes 4259840 | tf_op jit(solution)/shard_map/nrc,nr->nc/dot_general | solution.py:73
  67.3 11.1 %add_multiply_fusion.1 = (f32[16,128]{1,0:T(8,128)}, f32[16,128]{1,0:T(8,128)S(1)}) fusion(f32[16,128]{1,0:T(8,128)S(1)} %fusion.7, pred[16,128]{1,0:T(8,128)(4,1)S(1)} %get-tuple-element.16, pred[16,128]{1,0:T(8,128)(4,1)S(1)} %get-tuple-element.15, pred[16,128]{1,0:T(8,128)(4,1)S(1)} %get-tuple-element.14, pred[16,128]{1,0:T(8,128)(4,1)S(1)} %get-tuple-element.13, ...), kind=kOutput, calls=%fused_computation.57 | convolution fusion | flops 1629184 | bytes 82496 | tf_op jit(solution)/shard_map/dot_general | solution.py:76
  78.6 6.6 %fusion.68 = f32[64,1,128]{2,1,0:T(1,128)S(1)} fusion(f32[64,128,1]{1,2,0:T(1,128)S(1)} %bitcast.55, f32[64,128,128]{2,1,0:T(8,128)S(1)} %copy-done.1), kind=kOutput, calls=%fused_computation.88 | convolution fusion | flops 12582912 | bytes 4259840 | tf_op jit(solution)/shard_map/nrc,nc->nr/dot_general | solution.py:82
  85.5 1.9 %all-gather.1 = f32[192,128]{1,0:T(8,128)S(1)} all-gather(f32[96,128]{1,0:T(8,128)S(1)} %fusion.20), channel_id=3, replica_groups=mesh['grp'=2,'tm'=16] {'grp'}, dimensions={0}, use_global_device_ids=true | all-gather | bytes 147456 | tf_op jit(solution)/shard_map/all_gather | solution.py:86
  87.4 1.9 %collective-permute-start.6 = (f32[32,128]{1,0:T(8,128)S(1)}, f32[32,128]{1,0:T(8,128)S(1)}, u32[]{:S(2)}, u32[]{:S(2)}) collective-permute-start(f32[32,128]{1,0:T(8,128)S(1)} %get-tuple-element.6), channel_id=1, source_target_pairs={{1,0},{2,1},{3,2},{4,3},{5,4},{6,5},{7,6},{8,7},{9,8},{10,9},{11,1... | collective-permute-start | bytes 49160 | tf_op jit(solution)/shard_map/ppermute | solution.py:27
  89.3 3.9 %collective-permute-start.7 = (f32[32,128]{1,0:T(8,128)S(1)}, f32[32,128]{1,0:T(8,128)S(1)}, u32[]{:S(2)}, u32[]{:S(2)}) collective-permute-start(f32[32,128]{1,0:T(8,128)S(1)} %get-tuple-element.7), channel_id=1, source_target_pairs={{0,1},{1,2},{2,3},{3,4},{4,5},{5,6},{6,7},{7,8},{8,9},{9,10},{10,1... | collective-permute-start | bytes 49160 | tf_op jit(solution)/shard_map/ppermute | solution.py:27
  93.3 3.5 %collective-permute-done.7 = f32[32,128]{1,0:T(8,128)S(1)} collective-permute-done((f32[32,128]{1,0:T(8,128)S(1)}, f32[32,128]{1,0:T(8,128)S(1)}, u32[]{:S(2)}, u32[]{:S(2)}) %collective-permute-start.7) | collective-permute-done | bytes 16416 | tf_op jit(solution)/shard_map/ppermute | solution.py:27
  (32 shorter events, 2.7 us)
Async XLA Ops:
  0.6 18.9 %copy-start.5 = (f32[16,128]{1,0:T(8,128)S(1)}, f32[16,128]{1,0:T(8,128)}, u32[]{:S(2)}) copy-start(f32[16,128]{1,0:T(8,128)} %param.13) | copy-start | bytes 24580
  0.6 18.9 %copy-start.4 = (f32[16,128]{1,0:T(8,128)S(1)}, f32[16,128]{1,0:T(8,128)}, u32[]{:S(2)}) copy-start(f32[16,128]{1,0:T(8,128)} %param.11) | copy-start | bytes 24580
  0.7 12.6 %collective-permute-start.1 = (f32[32,128]{1,0:T(8,128)}, f32[32,128]{1,0:T(8,128)S(1)}, u32[]{:S(2)}, u32[]{:S(2)}) collective-permute-start(f32[32,128]{1,0:T(8,128)} %param.12), channel_id=1, source_target_pairs={{1,0},{2,1},{3,2},{4,3},{5,4},{6,5},{7,6},{8,7},{9,8},{10,9},{11,1... | collective-permute-start | bytes 49160 | tf_op jit(solution)/shard_map/ppermute | solution.py:19
  5.0 8.2 %collective-permute-start = (f32[32,128]{1,0:T(8,128)}, f32[32,128]{1,0:T(8,128)S(1)}, u32[]{:S(2)}, u32[]{:S(2)}) collective-permute-start(f32[32,128]{1,0:T(8,128)} %param.12), channel_id=1, source_target_pairs={{0,1},{1,2},{2,3},{3,4},{4,5},{5,6},{6,7},{7,8},{8,9},{9,10},{10,1... | collective-permute-start | bytes 49160 | tf_op jit(solution)/shard_map/ppermute | solution.py:16
  11.6 18.6 %copy-start = (f32[64,128,128]{2,1,0:T(8,128)S(1)}, f32[64,128,128]{2,1,0:T(8,128)}, u32[]{:S(2)}) copy-start(f32[64,128,128]{2,1,0:T(8,128)} %param.15) | copy-start | bytes 12582916
  14.2 38.2 %copy-start.2 = (f32[32,128]{1,0:T(8,128)S(1)}, f32[32,128]{1,0:T(8,128)}, u32[]{:S(2)}) copy-start(f32[32,128]{1,0:T(8,128)} %param.12) | copy-start | bytes 49156
  14.2 38.2 %copy-start.3 = (f32[32,128]{1,0:T(8,128)S(1)}, f32[32,128]{1,0:T(8,128)}, u32[]{:S(2)}) copy-start(f32[32,128]{1,0:T(8,128)} %param.14) | copy-start | bytes 49156
  39.0 39.6 %copy-start.1 = (f32[64,128,128]{2,1,0:T(8,128)S(1)}, f32[64,128,128]{2,1,0:T(8,128)}, u32[]{:S(2)}) copy-start(f32[64,128,128]{2,1,0:T(8,128)} %param.15) | copy-start | bytes 12582916
  39.0 7.9 %collective-permute-start.2 = (f32[32,128]{1,0:T(8,128)S(1)}, f32[32,128]{1,0:T(8,128)S(1)}, u32[]{:S(2)}, u32[]{:S(2)}) collective-permute-start(f32[32,128]{1,0:T(8,128)S(1)} %get-tuple-element.8), channel_id=1, source_target_pairs={{1,0},{2,1},{3,2},{4,3},{5,4},{6,5},{7,6},{8,7},{9,8},{10,9},{11,1... | collective-permute-start | bytes 49160 | tf_op jit(solution)/shard_map/ppermute | solution.py:27
  45.0 7.4 %collective-permute-start.3 = (f32[32,128]{1,0:T(8,128)S(1)}, f32[32,128]{1,0:T(8,128)S(1)}, u32[]{:S(2)}, u32[]{:S(2)}) collective-permute-start(f32[32,128]{1,0:T(8,128)S(1)} %get-tuple-element.9), channel_id=1, source_target_pairs={{0,1},{1,2},{2,3},{3,4},{4,5},{5,6},{6,7},{7,8},{8,9},{9,10},{10,1... | collective-permute-start | bytes 49160 | tf_op jit(solution)/shard_map/ppermute | solution.py:27
  52.4 6.0 %collective-permute-start.5 = (f32[32,128]{1,0:T(8,128)S(1)}, f32[32,128]{1,0:T(8,128)S(1)}, u32[]{:S(2)}, u32[]{:S(2)}) collective-permute-start(f32[32,128]{1,0:T(8,128)S(1)} %fusion.37), channel_id=1, source_target_pairs={{1,0},{2,1},{3,2},{4,3},{5,4},{6,5},{7,6},{8,7},{9,8},{10,9},{11,1... | collective-permute-start | bytes 49160 | tf_op jit(solution)/shard_map/ppermute | solution.py:19
  54.4 7.4 %collective-permute-start.4 = (f32[32,128]{1,0:T(8,128)S(1)}, f32[32,128]{1,0:T(8,128)S(1)}, u32[]{:S(2)}, u32[]{:S(2)}) collective-permute-start(f32[32,128]{1,0:T(8,128)S(1)} %fusion.37), channel_id=1, source_target_pairs={{0,1},{1,2},{2,3},{3,4},{4,5},{5,6},{6,7},{7,8},{8,9},{9,10},{10,1... | collective-permute-start | bytes 49160 | tf_op jit(solution)/shard_map/ppermute | solution.py:16
  78.4 19.0 %copy-start.6 = (f32[16,128]{1,0:T(8,128)}, f32[16,128]{1,0:T(8,128)S(1)}, u32[]{:S(2)}) copy-start(f32[16,128]{1,0:T(8,128)S(1)} %get-tuple-element.35) | copy-start | bytes 24580
  87.4 5.9 %collective-permute-start.6 = (f32[32,128]{1,0:T(8,128)S(1)}, f32[32,128]{1,0:T(8,128)S(1)}, u32[]{:S(2)}, u32[]{:S(2)}) collective-permute-start(f32[32,128]{1,0:T(8,128)S(1)} %get-tuple-element.6), channel_id=1, source_target_pairs={{1,0},{2,1},{3,2},{4,3},{5,4},{6,5},{7,6},{8,7},{9,8},{10,9},{11,1... | collective-permute-start | bytes 49160 | tf_op jit(solution)/shard_map/ppermute | solution.py:27
  89.3 7.4 %collective-permute-start.7 = (f32[32,128]{1,0:T(8,128)S(1)}, f32[32,128]{1,0:T(8,128)S(1)}, u32[]{:S(2)}, u32[]{:S(2)}) collective-permute-start(f32[32,128]{1,0:T(8,128)S(1)} %get-tuple-element.7), channel_id=1, source_target_pairs={{0,1},{1,2},{2,3},{3,4},{4,5},{5,6},{6,7},{7,8},{8,9},{9,10},{10,1... | collective-permute-start | bytes 49160 | tf_op jit(solution)/shard_map/ppermute | solution.py:27
